TPU v7x, 32 devices: a whole 2x2x4 slice. The times are simulated.
32 devices in a mesh: groups: 2 (over x), dp: 8 (over z, y), split: 2 (over core).
Axes of the slice: x: 2, y: 2, z: 4, core: 2. Of those that a mesh axis runs over, the one named last changes fastest.
Arguments:
- embeddings: bfloat16 [65536, 512], P(('groups', 'dp', 'split')), parts along dimension 0, may hold values from -6 to 6
- assignment: int32 [65536, 1], P(('groups', 'dp', 'split')), parts along dimension 0, may hold values from 0 to 15; in each aligned block of 2048 rows (0 to 2047, 2048 to 4095, ...) at most 192 rows name the same one
- order_key: int32 [65536], P(('groups', 'dp', 'split')), parts along dimension 0, may hold values from 0 to 32767, each once
Outputs:
- nearest: float32 [65536], P(('groups', 'dp', 'split')), parts along dimension 0
There are 2 independent parts, one for each index of `groups`. A program takes and returns all parts, laid end to end along the dimension named above; each array names one. Nothing has to cross between parts.
Inputs may be any that keep to these rules, and one draw needn't show every extreme that they name: `assignment`: in each device's 2048 rows no cluster has more than 192 rows, and some cluster has exactly 192. `order_key`: all values within a part are distinct.
All inputs are finite; a program needn't handle non-finite values.
Results may differ from a plain program's by a relative error of at most 0.0013.
Values may be sent and summed in bfloat16 or wider, within the bound.
A program may use at most 64 MiB of HBM per device.

v0:
```python
import functools

import jax
import jax.numpy as jnp
from jax import lax
from jax.experimental import pallas as pl
from jax.experimental.pallas import tpu as pltpu
from jax.sharding import PartitionSpec as P

epsilon = 1e-06
MESH = pl.DeviceIdType.MESH
NT = (((1,), (1,)), ((), ()))
BLOCK = 256
SUB = 8
GROUP = 5


def xor(a, b, n):
    total, bit = 0, 1
    while bit < n:
        p, q = (a // bit) % 2, (b // bit) % 2
        total = total + (p + q - 2 * p * q) * bit
        bit *= 2
    return total


def offset_of(slot, n):
    t = slot - 1
    h = n // 2
    far = slot // (h + 2)
    first = (h + 2 - slot) // h
    return (1 - far) * (first * (h + t) + (1 - first) * (t - 1)) + far * (slot % n)


def kernel(n, n_split, most, rows_hbm, cluster_ref, key_ref, out_ref,
           rows_ref, rows_sem, slot_ref, send, send_key, recv, recv_key, lane_key, sub_key, best, back_send, back, back_parts,
           row_ssem, row_rsem, key_ssem, key_rsem, back_ssem, back_rsem):
    f32, bf16, i32 = jnp.float32, jnp.bfloat16, jnp.int32
    rows = rows_ref.shape[0]
    fetch = pltpu.make_async_copy(rows_hbm, rows_ref, rows_sem)
    fetch.start()
    me = lax.axis_index("dp") * n_split + lax.axis_index("split")

    def device(slot):
        partner = xor(me, offset_of(slot, n), n)
        return {"dp": partner // n_split, "split": partner % n_split}

    barrier = pltpu.get_barrier_semaphore()

    @pl.loop(1, n)
    def _(slot):
        pl.semaphore_signal(barrier, inc=1, device_id=device(slot), device_id_type=MESH)

    before = (lax.broadcasted_iota(i32, (BLOCK, BLOCK), 0) < lax.broadcasted_iota(i32, (BLOCK, BLOCK), 1))
    before = jnp.where(before, 1.0, 0.0).astype(bf16)
    carry = jnp.zeros((n, 1), f32)
    for start in range(0, rows, BLOCK):
        here = cluster_ref[:, start:start + BLOCK]
        onehot = jnp.where(lax.broadcasted_iota(i32, (n, BLOCK), 0) == here, 1.0, 0.0)
        earlier = jnp.dot(onehot.astype(bf16), before, preferred_element_type=f32) + carry
        carry = carry + jnp.sum(onehot, axis=1, keepdims=True)
        rank = jnp.sum(onehot * earlier, axis=0, keepdims=True).astype(i32)
        slot_ref[:, start:start + BLOCK] = here * most + rank

    key = key_ref[...]
    digit = lax.broadcasted_iota(i32, (SUB, rows), 0)
    digits = jnp.where(digit == 0, key // 16384, jnp.where(digit == 1, (key // 128) % 128, jnp.where(digit == 2, key % 128, jnp.where(digit == 3, 1, 0))))
    digits = digits.astype(f32).astype(bf16)

    place = lax.broadcasted_iota(i32, (SUB, SUB), 1)
    combine = jnp.where(place == 0, 16384.0, jnp.where(place == 1, 128.0, jnp.where(place == 2, 1.0, jnp.where(place == 3, -4194304.0, 0.0)))).astype(bf16)
    part = lax.broadcasted_iota(i32, (SUB, most), 0)

    def parts_of(row):
        whole = jnp.broadcast_to(row, (SUB, most))
        high = whole.astype(bf16).astype(f32)
        middle = (whole - high).astype(bf16).astype(f32)
        low = (whole - high) - middle
        return jnp.where(part == 0, high, jnp.where(part == 1, middle, jnp.where(part == 2, low, 0.0)))

    same = lax.broadcasted_iota(i32, (most, most), 0) == lax.broadcasted_iota(i32, (most, most), 1)
    identity = jnp.where(same, 1.0, 0.0).astype(bf16)

    def pack(cluster):
        place = slot_ref[...] - cluster * most
        pick = jnp.where(lax.broadcasted_iota(i32, (most, rows), 0) == place, 1.0, 0.0).astype(bf16)
        values = jnp.dot(pick, rows_ref[...], preferred_element_type=f32)
        scale = lax.rsqrt(jnp.sum(values * values, axis=1, keepdims=True) + epsilon)
        picked = lax.dot_general(digits, pick, NT, preferred_element_type=f32)
        return (values * scale).astype(bf16), jnp.dot(combine, picked.astype(bf16), preferred_element_type=f32)[:1]

    def row_copy(slot):
        return pltpu.make_async_remote_copy(send.at[slot], recv.at[slot], row_ssem.at[slot], row_rsem.at[slot], device_id=device(slot), device_id_type=MESH)

    def key_copy(slot):
        return pltpu.make_async_remote_copy(send_key.at[slot], recv_key.at[slot], key_ssem.at[slot], key_rsem.at[slot], device_id=device(slot), device_id_type=MESH)

    def back_copy(slot, cluster):
        return pltpu.make_async_remote_copy(back_send.at[slot], back.at[cluster], back_ssem.at[slot], back_rsem.at[slot], device_id=device(slot), device_id_type=MESH)

    fetch.wait()
    send[1], send_key[1] = pack(xor(me, offset_of(1, n), n))
    pl.semaphore_wait(barrier, n - 1)

    @pl.loop(2, n + 1)
    def _(slot):
        row_copy(slot - 1).start()
        key_copy(slot - 1).start()
        at = slot % n
        packed, packed_key = pack(xor(me, offset_of(slot, n), n))
        send[at] = packed
        send_key[at] = packed_key

    def take(slot, row):
        lane_key[slot] = jnp.broadcast_to(row, (SUB, most))
        turned = lax.dot_general(identity, parts_of(row).astype(bf16), NT, preferred_element_type=f32).astype(bf16)
        sub_key[slot] = jnp.dot(turned, jnp.ones((SUB, most), bf16), preferred_element_type=f32)

    def tile(columns, columns_key, own, own_key):
        sims = lax.dot_general(columns, own, NT, preferred_element_type=f32)
        seen = jnp.where(columns_key < own_key, sims, -1.0)
        return jnp.max(seen.reshape(most // SUB, SUB, most), axis=0)

    recv[0] = send[0]
    take(0, send_key[0])
    best[0] = jnp.maximum(tile(recv[0], sub_key[0], recv[0], lane_key[0][:1]), -1.0)

    @pl.loop(1, n)
    def _(u):
        row_copy(u).wait_recv()
        key_copy(u).wait_recv()
        new = recv[u]
        take(u, recv_key[u])
        new_lane, new_sub = lane_key[u][:1], sub_key[u]

        def meet(i, running):
            other = recv[i]
            best[i] = jnp.maximum(best[i], tile(new, new_sub, other, lane_key[i][:1]))
            return jnp.maximum(running, tile(other, sub_key[i], new, new_lane))

        def meet_group(group, running):
            for i in range(GROUP):
                running = meet(group * GROUP + i, running)
            return running

        running = lax.fori_loop(0, u // GROUP, meet_group, tile(new, new_sub, new, new_lane))
        best[u] = lax.fori_loop(u // GROUP * GROUP, u, meet, running)

    back_send[n - 1] = jnp.max(best[n - 1], axis=0, keepdims=True)

    @pl.loop(2, n)
    def _(step):
        back_send[n - step] = jnp.max(best[n - step], axis=0, keepdims=True)
        back_copy(n - step + 1, me).start()

    back_copy(1, me).start()
    back_parts[me] = parts_of(jnp.max(best[0], axis=0, keepdims=True))

    @pl.loop(1, n)
    def _(slot):
        row_copy(slot).wait_send()
        key_copy(slot).wait_send()

    @pl.loop(1, n)
    def _(slot):
        cluster = xor(me, offset_of(slot, n), n)
        back_copy(slot, cluster).wait_recv()
        back_parts[cluster] = parts_of(back[cluster])

    turned = lax.dot_general(identity, back_parts[...].reshape(n * SUB, most).astype(bf16), NT, preferred_element_type=f32).astype(bf16)
    for start in range(0, rows, BLOCK):
        here = cluster_ref[:, start:start + BLOCK]
        rank = slot_ref[:, start:start + BLOCK] - here * most
        onehot = jnp.where(lax.broadcasted_iota(i32, (n * SUB, BLOCK), 0) // SUB == here, 1.0, 0.0).astype(bf16)
        found = jnp.dot(turned, onehot, preferred_element_type=f32)
        found = jnp.where(lax.broadcasted_iota(i32, (most, BLOCK), 0) == rank, found, 0.0)
        out_ref[:, start:start + BLOCK] = jnp.sum(found, axis=0, keepdims=True)

    @pl.loop(1, n)
    def _(slot):
        back_copy(slot, me).wait_send()


def per_device(embeddings, assignment, order_key):
    rows, width = embeddings.shape
    n_split = lax.axis_size("split")
    n = lax.axis_size("dp") * n_split
    most = 3 * rows // (2 * n)
    f32, bf16 = jnp.float32, jnp.bfloat16
    vmem = pl.BlockSpec(memory_space=pltpu.VMEM)
    dma = pltpu.SemaphoreType.DMA((n,))
    nearest = pl.pallas_call(
        functools.partial(kernel, n, n_split, most),
        out_shape=jax.ShapeDtypeStruct((1, rows), f32),
        in_specs=[pl.BlockSpec(memory_space=pl.ANY), vmem, vmem],
        out_specs=vmem,
        scratch_shapes=[
            pltpu.VMEM((rows, width), bf16),
            pltpu.SemaphoreType.DMA,
            pltpu.VMEM((1, rows), jnp.int32),
            pltpu.VMEM((n, most, width), bf16),
            pltpu.VMEM((n, 1, most), f32),
            pltpu.VMEM((n, most, width), bf16),
            pltpu.VMEM((n, 1, most), f32),
            pltpu.VMEM((n, SUB, most), f32),
            pltpu.VMEM((n, most, most), f32),
            pltpu.VMEM((n, SUB, most), f32),
            pltpu.VMEM((n, 1, most), f32),
            pltpu.VMEM((n, 1, most), f32),
            pltpu.VMEM((n, SUB, most), f32),
            dma, dma, dma, dma, dma, dma,
        ],
        compiler_params=pltpu.CompilerParams(collective_id=0, has_side_effects=True, vmem_limit_bytes=56 * 1024 * 1024),
    )(embeddings, assignment.reshape(1, rows), order_key.reshape(1, rows))
    return nearest.reshape(rows)


def solution(mesh):
    placed = (
        P(("groups", "dp", "split"), None),
        P(("groups", "dp", "split"), None),
        P(("groups", "dp", "split")),
    )
    return jax.shard_map(
        per_device,
        mesh=mesh,
        in_specs=placed,
        out_specs=P(("groups", "dp", "split")),
        check_vma=False,
    )
```

profile of v0, /device:TPU:0, one launch (start us, length us, event | category | flops | bytes accessed | tf_op | source)
XLA Modules:
  0.0 86.8 jit_solution(1951884632496194151)
XLA Ops:
  0.0 85.5 %shard_map.37 = f32[1,2048]{1,0:T(1,128)} custom-call(bf16[2048,512]{1,0:T(8,128)(2,1)} %rows_hbm.1, s32[1,2048]{1,0:T(1,128)} %bitcast.4, s32[1,2048]{1,0:T(1,128)} %bitcast.5), custom_call_target="tpu_custom_call" | custom-call | tf_op jit(solution)/shard_map/pallas_call | solution.py:192
  85.5 1.3 %copy.5 = f32[2048]{0:T(1024)} copy(f32[2048]{0:T(1024)} %bitcast.3) | data formatting | bytes 16384
where the time goes:
time: 87.1 us; the launch traced here: 86.8 us
  Pallas kernels  85.5 us (98%)
  local copies, waits for them, and re-layouts  1.3 us (1%)
    pallas_call x1, Pallas kernels, per_device(): pl.pallas_call(functools.partial(kernel, n, n_split, most), out_shape=jax...  85.5 us

commit v1 on v0

v1 whole, which is shorter than its diff:
```python
import functools

import jax
import jax.numpy as jnp
from jax import lax
from jax.experimental import pallas as pl
from jax.experimental.pallas import tpu as pltpu
from jax.sharding import PartitionSpec as P

epsilon = 1e-06
MESH = pl.DeviceIdType.MESH
NT = (((1,), (1,)), ((), ()))
BLOCK = 256
SUB = 8
GROUP = 5


def xor(a, b, n):
    total, bit = 0, 1
    while bit < n:
        p, q = (a // bit) % 2, (b // bit) % 2
        total = total + (p + q - 2 * p * q) * bit
        bit *= 2
    return total


def flip(a, b, n):
    total, bit = 0, 1
    while bit < n:
        p = (a // bit) % 2
        total = total + (1 - p if b & bit else p) * bit
        bit *= 2
    return total


def entry(values, i):
    n, total = len(values), values[0] + i
    for k in range(1, n):
        jump = values[k] - values[k - 1] - 1
        if jump:
            total = total + jump * lax.div(i + (n - k), n)
    return total


def orders(n):
    q = n // 4
    same, near, far2, far3 = (list(range(max(1, i * q), i * q + q)) for i in range(4))
    send_outer = far2 + same + near + far3
    send_inner = far3[:2] + far2 + same + near + far3[2:]
    take_outer = [0] + same + near + far2 + far3
    take_inner = [0] + same + far3[:2] + far2 + near + far3[2:]
    return send_outer + [0], send_inner + [0], take_outer, take_inner


def kernel(n, n_split, most, rows_hbm, cluster_hbm, key_hbm, out_ref,
           rows_ref, cluster_ref, key_ref, fetch_sem, slot_ref, send, send_key, recv, recv_key, lane_key, sub_key, best, gather, back_send, back, by_rank,
           row_ssem, row_rsem, key_ssem, key_rsem, back_ssem, back_rsem, go):
    f32, bf16, i32 = jnp.float32, jnp.bfloat16, jnp.int32
    rows = rows_ref.shape[0]
    quarter = n // 4
    me = lax.axis_index("dp") * n_split + lax.axis_index("split")
    inner = (me // quarter // 2 + me // quarter) % 2
    barrier = pltpu.get_barrier_semaphore()

    def place_of(partner):
        return {"dp": partner // n_split, "split": partner % n_split}

    def device(offset):
        return place_of(flip(me, offset, n) if isinstance(offset, int) else xor(me, offset, n))

    def greet(offset):
        pl.semaphore_signal(barrier, inc=1, device_id=device(offset), device_id_type=MESH)

    @pl.when(inner == 1)
    def _():
        for offset in [3 * quarter, 3 * quarter + 1] + list(range(3 * quarter - 1, quarter - 1, -1)):
            greet(offset)

    @pl.when(inner == 0)
    def _():
        for offset in list(range(n - 1, 3 * quarter - 1, -1)) + list(range(1, quarter)):
            greet(offset)

    fetches = [
        pltpu.make_async_copy(cluster_hbm, cluster_ref, fetch_sem.at[0]),
        pltpu.make_async_copy(key_hbm, key_ref, fetch_sem.at[1]),
        pltpu.make_async_copy(rows_hbm, rows_ref, fetch_sem.at[2]),
    ]
    for fetch in fetches:
        fetch.start()

    send_outer, send_inner, take_outer, take_inner = orders(n)

    def either(outer_values, inner_values, i):
        first, second = entry(outer_values, i), entry(inner_values, i)
        return first + (second - first) * inner

    def sent(i):
        return either(send_outer, send_inner, i)

    def taken(i):
        return either(take_outer, take_inner, i)

    fetches[0].wait()
    before = (lax.broadcasted_iota(i32, (BLOCK, BLOCK), 0) < lax.broadcasted_iota(i32, (BLOCK, BLOCK), 1))
    before = jnp.where(before, 1.0, 0.0).astype(bf16)
    carry = jnp.zeros((n, 1), f32)
    for start in range(0, rows, BLOCK):
        here = cluster_ref[:, start:start + BLOCK]
        onehot = jnp.where(lax.broadcasted_iota(i32, (n, BLOCK), 0) == here, 1.0, 0.0)
        earlier = jnp.dot(onehot.astype(bf16), before, preferred_element_type=f32) + carry
        carry = carry + jnp.sum(onehot, axis=1, keepdims=True)
        rank = jnp.sum(onehot * earlier, axis=0, keepdims=True).astype(i32)
        slot_ref[:, start:start + BLOCK] = here * most + rank

    fetches[1].wait()
    key = key_ref[...]
    digit = lax.broadcasted_iota(i32, (SUB, rows), 0)
    digits = jnp.where(digit == 0, key // 16384, jnp.where(digit == 1, (key // 128) % 128, jnp.where(digit == 2, key % 128, jnp.where(digit == 3, 1, 0))))
    digits = digits.astype(f32).astype(bf16)

    place = lax.broadcasted_iota(i32, (SUB, SUB), 1)
    combine = jnp.where(place == 0, 16384.0, jnp.where(place == 1, 128.0, jnp.where(place == 2, 1.0, jnp.where(place == 3, -4194304.0, 0.0)))).astype(bf16)
    part = lax.broadcasted_iota(i32, (SUB, most), 0)

    def split3(whole):
        high = whole.astype(bf16).astype(f32)
        middle = (whole - high).astype(bf16).astype(f32)
        return high, middle, (whole - high) - middle

    def parts_of(row):
        high, middle, low = split3(jnp.broadcast_to(row, (SUB, most)))
        return jnp.where(part == 0, high, jnp.where(part == 1, middle, jnp.where(part == 2, low, 0.0)))

    same = lax.broadcasted_iota(i32, (most, most), 0) == lax.broadcasted_iota(i32, (most, most), 1)
    identity = jnp.where(same, 1.0, 0.0).astype(bf16)

    def pack(cluster):
        place = slot_ref[...] - cluster * most
        pick = jnp.where(lax.broadcasted_iota(i32, (most, rows), 0) == place, 1.0, 0.0).astype(bf16)
        values = jnp.dot(pick, rows_ref[...], preferred_element_type=f32)
        scale = lax.rsqrt(jnp.sum(values * values, axis=1, keepdims=True) + epsilon)
        picked = lax.dot_general(digits, pick, NT, preferred_element_type=f32)
        return (values * scale).astype(bf16), jnp.dot(combine, picked.astype(bf16), preferred_element_type=f32)[:1]

    def row_copy(offset):
        return pltpu.make_async_remote_copy(send.at[offset], recv.at[offset], row_ssem.at[offset], row_rsem.at[offset], device_id=device(offset), device_id_type=MESH)

    def key_copy(offset):
        return pltpu.make_async_remote_copy(send_key.at[offset], recv_key.at[offset], key_ssem.at[offset], key_rsem.at[offset], device_id=device(offset), device_id_type=MESH)

    def back_copy(offset, cluster):
        return pltpu.make_async_remote_copy(back_send.at[offset], back.at[cluster], back_ssem.at[offset], back_rsem.at[offset], device_id=device(offset), device_id_type=MESH)

    def fill(step):
        offset = sent(step)
        packed, packed_key = pack(xor(me, offset, n))
        send[offset] = packed
        send_key[offset] = packed_key

    fetches[2].wait()
    fill(jnp.int32(0))

    @pl.when(inner == 1)
    def _():
        pl.semaphore_wait(barrier, 2)

    @pl.when(inner == 0)
    def _():
        pl.semaphore_wait(barrier, n - 1)
        pl.semaphore_signal(go, inc=1, device_id=device(quarter), device_id_type=MESH)

    @pl.loop(1, n)
    def _(step):
        @pl.when(inner * step == 3)
        def _():
            pl.semaphore_wait(go, 1)

        offset = sent(step - 1)
        key_copy(offset).start()
        row_copy(offset).start()
        fill(step)

    for start in range(0, rows, BLOCK):
        rank = slot_ref[:, start:start + BLOCK] - cluster_ref[:, start:start + BLOCK] * most
        by_rank[:, start:start + BLOCK] = jnp.where(lax.broadcasted_iota(i32, (most, BLOCK), 0) == rank, 1.0, 0.0).astype(bf16)

    def take(offset, row):
        lane_key[offset] = jnp.broadcast_to(row, (SUB, most))
        turned = lax.dot_general(identity, parts_of(row).astype(bf16), NT, preferred_element_type=f32).astype(bf16)
        sub_key[...] = jnp.dot(turned, jnp.ones((SUB, most), bf16), preferred_element_type=f32)

    def highest(values):
        return jnp.max(values.reshape(most // SUB, SUB, most), axis=0)

    def alone(offset):
        block = recv[offset]
        sims = lax.dot_general(block, block, NT, preferred_element_type=f32)
        best[offset] = highest(jnp.where(sub_key[...] < lane_key[offset][:1], sims, -1.0))

    recv[0] = send[0]
    take(0, send_key[0])
    alone(0)

    @pl.loop(1, n)
    def _(step):
        u = taken(step)
        key_copy(u).wait_recv()
        take(u, recv_key[u])
        row_copy(u).wait_recv()
        alone(u)
        gather[...] = jnp.full((most, most), -1.0, f32)

        def meet(i):
            other = taken(i)
            sims = lax.dot_general(recv[u], recv[other], NT, preferred_element_type=f32)
            earlier = sub_key[...] < lane_key[other][:1]
            best[other] = jnp.maximum(best[other], highest(jnp.where(earlier, sims, -1.0)))
            return jnp.where(earlier, -1.0, sims)

        @pl.loop(0, step // GROUP)
        def _(group):
            seen = meet(group * GROUP)
            for i in range(1, GROUP):
                seen = jnp.maximum(seen, meet(group * GROUP + i))
            gather[...] = jnp.maximum(gather[...], seen)

        @pl.loop(step // GROUP * GROUP, step)
        def _(i):
            gather[...] = jnp.maximum(gather[...], meet(i))

        best[u] = jnp.maximum(best[u], highest(gather[...].T))

    for offset in range(n - 1, 0, -1):
        back_send[offset] = jnp.max(best[offset], axis=0, keepdims=True)
        back_copy(offset, me).start()
    back[me] = jnp.max(best[0], axis=0, keepdims=True)

    @pl.loop(1, n)
    def _(offset):
        row_copy(offset).wait_send()
        key_copy(offset).wait_send()

    for offset in range(1, n):
        back_copy(offset, flip(me, offset, n)).wait_recv()

    parts = jnp.concatenate(split3(back[...].reshape(n, most)), axis=0).astype(bf16)
    for start in range(0, rows, BLOCK):
        here = cluster_ref[:, start:start + BLOCK]
        found = jnp.dot(parts, by_rank[:, start:start + BLOCK], preferred_element_type=f32)
        whole = found[:n] + found[n:2 * n] + found[2 * n:]
        whole = jnp.where(lax.broadcasted_iota(i32, (n, BLOCK), 0) == here, whole, 0.0)
        out_ref[:, start:start + BLOCK] = jnp.sum(whole, axis=0, keepdims=True)

    for offset in range(1, n):
        back_copy(offset, me).wait_send()


def per_device(embeddings, assignment, order_key):
    rows, width = embeddings.shape
    n_split = lax.axis_size("split")
    n = lax.axis_size("dp") * n_split
    most = 3 * rows // (2 * n)
    f32, bf16 = jnp.float32, jnp.bfloat16
    vmem = pl.BlockSpec(memory_space=pltpu.VMEM)
    dma = pltpu.SemaphoreType.DMA((n,))
    nearest = pl.pallas_call(
        functools.partial(kernel, n, n_split, most),
        out_shape=jax.ShapeDtypeStruct((1, rows), f32),
        in_specs=[pl.BlockSpec(memory_space=pl.ANY)] * 3,
        out_specs=vmem,
        scratch_shapes=[
            pltpu.VMEM((rows, width), bf16),
            pltpu.VMEM((1, rows), jnp.int32),
            pltpu.VMEM((1, rows), jnp.int32),
            pltpu.SemaphoreType.DMA((3,)),
            pltpu.VMEM((1, rows), jnp.int32),
            pltpu.VMEM((n, most, width), bf16),
            pltpu.VMEM((n, 1, most), f32),
            pltpu.VMEM((n, most, width), bf16),
            pltpu.VMEM((n, 1, most), f32),
            pltpu.VMEM((n, SUB, most), f32),
            pltpu.VMEM((most, most), f32),
            pltpu.VMEM((n, SUB, most), f32),
            pltpu.VMEM((most, most), f32),
            pltpu.VMEM((n, 1, most), f32),
            pltpu.VMEM((n, 1, most), f32),
            pltpu.VMEM((most, rows), bf16),
            dma, dma, dma, dma, dma, dma,
            pltpu.SemaphoreType.REGULAR,
        ],
        compiler_params=pltpu.CompilerParams(collective_id=0, has_side_effects=True, vmem_limit_bytes=56 * 1024 * 1024),
    )(embeddings, assignment.reshape(1, rows), order_key.reshape(1, rows))
    return nearest.reshape(rows)


def solution(mesh):
    placed = (
        P(("groups", "dp", "split"), None),
        P(("groups", "dp", "split"), None),
        P(("groups", "dp", "split")),
    )
    return jax.shard_map(
        per_device,
        mesh=mesh,
        in_specs=placed,
        out_specs=P(("groups", "dp", "split")),
        check_vma=False,
    )
```

time: 87.1 us -> 84.6 us (0.971)
  Pallas kernels: 85.5 us -> 83 us
    pallas_call x1, Pallas kernels: 85.5 us -> 83 us  [per_device(): pl.pallas_call(functools.partial(kernel, n, n_split, most), out_shape=jax...]
where the time goes in v1:
time: 84.6 us; the launch traced here: 84.3 us
  Pallas kernels  83 us (98%)
  local copies, waits for them, and re-layouts  1.3 us (2%)
    pallas_call x1, Pallas kernels, per_device(): pl.pallas_call(functools.partial(kernel, n, n_split, most), out_shape=jax...  83 us

profile of v1, /device:TPU:0, one launch (start us, length us, event | category | flops | bytes accessed | tf_op | source)
XLA Modules:
  0.0 84.3 jit_solution(15119331981126161926)
XLA Ops:
  0.0 83.0 %shard_map.37 = f32[1,2048]{1,0:T(1,128)} custom-call(bf16[2048,512]{1,0:T(8,128)(2,1)} %rows_hbm.1, s32[1,2048]{1,0:T(1,128)} %bitcast.4, s32[1,2048]{1,0:T(1,128)} %bitcast.5), custom_call_target="tpu_custom_call" | custom-call | tf_op jit(solution)/shard_map/pallas_call | solution.py:267
  83.0 1.3 %copy.5 = f32[2048]{0:T(1024)} copy(f32[2048]{0:T(1024)} %bitcast.3) | data formatting | bytes 16384

commit v2 on v1

--- a/solution.py
+++ b/solution.py
@@ -47,8 +47,8 @@
     same, near, far2, far3 = (list(range(max(1, i * q), i * q + q)) for i in range(4))
     send_outer = far2 + same + near + far3
     send_inner = far3[:2] + far2 + same + near + far3[2:]
-    take_outer = [0] + same + near + far2 + far3
-    take_inner = [0] + same + far3[:2] + far2 + near + far3[2:]
+    take_outer = [0] + same + near + far2[:q // 2] + far3 + far2[q // 2:]
+    take_inner = [0] + same[:1] + far2[:-1] + same[1:-1] + far2[-1:] + far3[:1] + near[:1] + same[-1:] + far3[1:2] + near[1:] + far3[2:]
     return send_outer + [0], send_inner + [0], take_outer, take_inner
 
 
@@ -71,16 +71,6 @@
     def greet(offset):
         pl.semaphore_signal(barrier, inc=1, device_id=device(offset), device_id_type=MESH)
 
-    @pl.when(inner == 1)
-    def _():
-        for offset in [3 * quarter, 3 * quarter + 1] + list(range(3 * quarter - 1, quarter - 1, -1)):
-            greet(offset)
-
-    @pl.when(inner == 0)
-    def _():
-        for offset in list(range(n - 1, 3 * quarter - 1, -1)) + list(range(1, quarter)):
-            greet(offset)
-
     fetches = [
         pltpu.make_async_copy(cluster_hbm, cluster_ref, fetch_sem.at[0]),
         pltpu.make_async_copy(key_hbm, key_ref, fetch_sem.at[1]),
@@ -88,6 +78,16 @@
     ]
     for fetch in fetches:
         fetch.start()
+
+    @pl.when(inner == 1)
+    def _():
+        for offset in [3 * quarter, 3 * quarter + 1] + list(range(3 * quarter - 1, quarter - 1, -1)):
+            greet(offset)
+
+    @pl.when(inner == 0)
+    def _():
+        for offset in list(range(n - 1, 3 * quarter - 1, -1)) + list(range(1, quarter)):
+            greet(offset)
 
     send_outer, send_inner, take_outer, take_inner = orders(n)
 
@@ -231,10 +231,10 @@
 
         best[u] = jnp.maximum(best[u], highest(gather[...].T))
 
+    back_send[...] = jnp.max(best[...], axis=1, keepdims=True)
+    back[me] = jnp.max(best[0], axis=0, keepdims=True)
     for offset in range(n - 1, 0, -1):
-        back_send[offset] = jnp.max(best[offset], axis=0, keepdims=True)
         back_copy(offset, me).start()
-    back[me] = jnp.max(best[0], axis=0, keepdims=True)
 
     @pl.loop(1, n)
     def _(offset):
@@ -266,7 +266,7 @@
     dma = pltpu.SemaphoreType.DMA((n,))
     nearest = pl.pallas_call(
         functools.partial(kernel, n, n_split, most),
-        out_shape=jax.ShapeDtypeStruct((1, rows), f32),
+        out_shape=pltpu.VMEM((1, rows), f32),
         in_specs=[pl.BlockSpec(memory_space=pl.ANY)] * 3,
         out_specs=vmem,
         scratch_shapes=[

time: 84.6 us -> 81.6 us (0.965)
  Pallas kernels: 83 us -> 80.8 us
    pallas_call x1, Pallas kernels: 83 us -> 80.8 us  [per_device(): pl.pallas_call(functools.partial(kernel, n, n_split, most), out_shape=plt...]
where the time goes in v2:
time: 81.6 us; the launch traced here: 81.4 us
  Pallas kernels  80.8 us (99%)
    pallas_call x1, Pallas kernels, per_device(): pl.pallas_call(functools.partial(kernel, n, n_split, most), out_shape=plt...  80.8 us

profile of v2, /device:TPU:0, one launch (start us, length us, event | category | flops | bytes accessed | tf_op | source)
XLA Modules:
  0.0 81.4 jit_solution(4771224607064561104)
XLA Ops:
  0.0 80.8 %shard_map.37 = f32[1,2048]{1,0:T(1,128)S(1)} custom-call(bf16[2048,512]{1,0:T(8,128)(2,1)} %rows_hbm.1, s32[1,2048]{1,0:T(1,128)} %bitcast.4, s32[1,2048]{1,0:T(1,128)} %bitcast.5), custom_call_target="tpu_custom_call" | custom-call | tf_op jit(solution)/shard_map/pallas_call | solution.py:267
  80.8 0.6 copy.5

commit v3 on v2

--- a/solution.py
+++ b/solution.py
@@ -13,6 +13,7 @@
 BLOCK = 256
 SUB = 8
 GROUP = 5
+PARTS = 2
 
 
 def xor(a, b, n):
@@ -48,7 +49,7 @@
     send_outer = far2 + same + near + far3
     send_inner = far3[:2] + far2 + same + near + far3[2:]
     take_outer = [0] + same + near + far2[:q // 2] + far3 + far2[q // 2:]
-    take_inner = [0] + same[:1] + far2[:-1] + same[1:-1] + far2[-1:] + far3[:1] + near[:1] + same[-1:] + far3[1:2] + near[1:] + far3[2:]
+    take_inner = [0] + same[:1] + far2 + same[1:] + far3[:2] + near + far3[2:]
     return send_outer + [0], send_inner + [0], take_outer, take_inner
 
 
@@ -71,10 +72,13 @@
     def greet(offset):
         pl.semaphore_signal(barrier, inc=1, device_id=device(offset), device_id_type=MESH)
 
+    part_rows = rows // PARTS
     fetches = [
         pltpu.make_async_copy(cluster_hbm, cluster_ref, fetch_sem.at[0]),
         pltpu.make_async_copy(key_hbm, key_ref, fetch_sem.at[1]),
-        pltpu.make_async_copy(rows_hbm, rows_ref, fetch_sem.at[2]),
+    ] + [
+        pltpu.make_async_copy(rows_hbm.at[pl.ds(i * part_rows, part_rows)], rows_ref.at[pl.ds(i * part_rows, part_rows)], fetch_sem.at[2 + i])
+        for i in range(PARTS)
     ]
     for fetch in fetches:
         fetch.start()
@@ -135,10 +139,17 @@
     same = lax.broadcasted_iota(i32, (most, most), 0) == lax.broadcasted_iota(i32, (most, most), 1)
     identity = jnp.where(same, 1.0, 0.0).astype(bf16)
 
-    def pack(cluster):
+    def pack(cluster, waits=()):
         place = slot_ref[...] - cluster * most
         pick = jnp.where(lax.broadcasted_iota(i32, (most, rows), 0) == place, 1.0, 0.0).astype(bf16)
-        values = jnp.dot(pick, rows_ref[...], preferred_element_type=f32)
+        if waits:
+            values = jnp.zeros((most, rows_ref.shape[1]), f32)
+            for i, wait in enumerate(waits):
+                wait()
+                part = slice(i * part_rows, (i + 1) * part_rows)
+                values = values + jnp.dot(pick[:, part], rows_ref[part], preferred_element_type=f32)
+        else:
+            values = jnp.dot(pick, rows_ref[...], preferred_element_type=f32)
         scale = lax.rsqrt(jnp.sum(values * values, axis=1, keepdims=True) + epsilon)
         picked = lax.dot_general(digits, pick, NT, preferred_element_type=f32)
         return (values * scale).astype(bf16), jnp.dot(combine, picked.astype(bf16), preferred_element_type=f32)[:1]
@@ -152,14 +163,13 @@
     def back_copy(offset, cluster):
         return pltpu.make_async_remote_copy(back_send.at[offset], back.at[cluster], back_ssem.at[offset], back_rsem.at[offset], device_id=device(offset), device_id_type=MESH)
 
-    def fill(step):
+    def fill(step, waits=()):
         offset = sent(step)
-        packed, packed_key = pack(xor(me, offset, n))
+        packed, packed_key = pack(xor(me, offset, n), waits)
         send[offset] = packed
         send_key[offset] = packed_key
 
-    fetches[2].wait()
-    fill(jnp.int32(0))
+    fill(jnp.int32(0), [fetch.wait for fetch in fetches[2:]])
 
     @pl.when(inner == 1)
     def _():
@@ -273,7 +283,7 @@
             pltpu.VMEM((rows, width), bf16),
             pltpu.VMEM((1, rows), jnp.int32),
             pltpu.VMEM((1, rows), jnp.int32),
-            pltpu.SemaphoreType.DMA((3,)),
+            pltpu.SemaphoreType.DMA((2 + PARTS,)),
             pltpu.VMEM((1, rows), jnp.int32),
             pltpu.VMEM((n, most, width), bf16),
             pltpu.VMEM((n, 1, most), f32),

time: 81.6 us -> 81.5 us (level)
  no operation moved by 1% of the time
where the time goes in v3:
time: 81.5 us; the launch traced here: 81.3 us
  Pallas kernels  80.7 us (99%)
    pallas_call x1, Pallas kernels, per_device(): pl.pallas_call(functools.partial(kernel, n, n_split, most), out_shape=plt...  80.7 us

profile of v3, /device:TPU:0, one launch (start us, length us, event | category | flops | bytes accessed | tf_op | source)
XLA Modules:
  0.0 81.3 jit_solution(7236026043962301384)
XLA Ops:
  0.0 80.7 %shard_map.37 = f32[1,2048]{1,0:T(1,128)S(1)} custom-call(bf16[2048,512]{1,0:T(8,128)(2,1)} %rows_hbm.1, s32[1,2048]{1,0:T(1,128)} %bitcast.4, s32[1,2048]{1,0:T(1,128)} %bitcast.5), custom_call_target="tpu_custom_call" | custom-call | tf_op jit(solution)/shard_map/pallas_call | solution.py:277
  80.7 0.6 copy.5

commit v4 on v3

--- a/solution.py
+++ b/solution.py
@@ -151,8 +151,11 @@
         else:
             values = jnp.dot(pick, rows_ref[...], preferred_element_type=f32)
         scale = lax.rsqrt(jnp.sum(values * values, axis=1, keepdims=True) + epsilon)
+        return (values * scale).astype(bf16), pick
+
+    def keys_of(pick):
         picked = lax.dot_general(digits, pick, NT, preferred_element_type=f32)
-        return (values * scale).astype(bf16), jnp.dot(combine, picked.astype(bf16), preferred_element_type=f32)[:1]
+        return jnp.dot(combine, picked.astype(bf16), preferred_element_type=f32)[:1]
 
     def row_copy(offset):
         return pltpu.make_async_remote_copy(send.at[offset], recv.at[offset], row_ssem.at[offset], row_rsem.at[offset], device_id=device(offset), device_id_type=MESH)
@@ -165,11 +168,12 @@
 
     def fill(step, waits=()):
         offset = sent(step)
-        packed, packed_key = pack(xor(me, offset, n), waits)
+        packed, pick = pack(xor(me, offset, n), waits)
         send[offset] = packed
-        send_key[offset] = packed_key
-
-    fill(jnp.int32(0), [fetch.wait for fetch in fetches[2:]])
+        return pick
+
+    first = sent(jnp.int32(0))
+    pick = fill(jnp.int32(0), [fetch.wait for fetch in fetches[2:]])
 
     @pl.when(inner == 1)
     def _():
@@ -179,6 +183,9 @@
     def _():
         pl.semaphore_wait(barrier, n - 1)
         pl.semaphore_signal(go, inc=1, device_id=device(quarter), device_id_type=MESH)
+
+    row_copy(first).start()
+    send_key[first] = keys_of(pick)
 
     @pl.loop(1, n)
     def _(step):
@@ -188,8 +195,12 @@
 
         offset = sent(step - 1)
         key_copy(offset).start()
-        row_copy(offset).start()
-        fill(step)
+
+        @pl.when(step > 1)
+        def _():
+            row_copy(offset).start()
+
+        send_key[sent(step)] = keys_of(fill(step))
 
     for start in range(0, rows, BLOCK):
         rank = slot_ref[:, start:start + BLOCK] - cluster_ref[:, start:start + BLOCK] * most

time: 81.5 us -> 89.6 us (1.099)
  Pallas kernels: 80.7 us -> 88.8 us
    pallas_call x1, Pallas kernels: 80.7 us -> 88.8 us  [per_device(): pl.pallas_call(functools.partial(kernel, n, n_split, most), out_shape=plt...]
where the time goes in v4:
time: 89.6 us; the launch traced here: 89.4 us
  Pallas kernels  88.8 us (99%)
    pallas_call x1, Pallas kernels, per_device(): pl.pallas_call(functools.partial(kernel, n, n_split, most), out_shape=plt...  88.8 us

profile of v4, /device:TPU:0, one launch (start us, length us, event | category | flops | bytes accessed | tf_op | source)
XLA Modules:
  0.0 89.4 jit_solution(6397618816648865550)
XLA Ops:
  0.0 88.8 %shard_map.37 = f32[1,2048]{1,0:T(1,128)S(1)} custom-call(bf16[2048,512]{1,0:T(8,128)(2,1)} %rows_hbm.1, s32[1,2048]{1,0:T(1,128)} %bitcast.4, s32[1,2048]{1,0:T(1,128)} %bitcast.5), custom_call_target="tpu_custom_call" | custom-call | tf_op jit(solution)/shard_map/pallas_call | solution.py:288
  88.8 0.6 copy.5

commit v5 on v3

--- a/solution.py
+++ b/solution.py
@@ -180,16 +180,19 @@
         pl.semaphore_wait(barrier, n - 1)
         pl.semaphore_signal(go, inc=1, device_id=device(quarter), device_id_type=MESH)
 
-    @pl.loop(1, n)
-    def _(step):
-        @pl.when(inner * step == 3)
-        def _():
-            pl.semaphore_wait(go, 1)
-
+    def advance(step):
         offset = sent(step - 1)
         key_copy(offset).start()
         row_copy(offset).start()
         fill(step)
+
+    pl.loop(1, 3)(advance)
+
+    @pl.when(inner == 1)
+    def _():
+        pl.semaphore_wait(go, 1)
+
+    pl.loop(3, n)(advance)
 
     for start in range(0, rows, BLOCK):
         rank = slot_ref[:, start:start + BLOCK] - cluster_ref[:, start:start + BLOCK] * most

time: 81.5 us -> 81.5 us (level)
  no operation moved by 1% of the time
where the time goes in v5:
time: 81.5 us; the launch traced here: 81.3 us
  Pallas kernels  80.7 us (99%)
    pallas_call x1, Pallas kernels, per_device(): pl.pallas_call(functools.partial(kernel, n, n_split, most), out_shape=plt...  80.7 us

profile of v5, /device:TPU:0, one launch (start us, length us, event | category | flops | bytes accessed | tf_op | source)
XLA Modules:
  0.0 81.3 jit_solution(4644617133409002798)
XLA Ops:
  0.0 80.7 %shard_map.37 = f32[1,2048]{1,0:T(1,128)S(1)} custom-call(bf16[2048,512]{1,0:T(8,128)(2,1)} %rows_hbm.1, s32[1,2048]{1,0:T(1,128)} %bitcast.4, s32[1,2048]{1,0:T(1,128)} %bitcast.5), custom_call_target="tpu_custom_call" | custom-call | tf_op jit(solution)/shard_map/pallas_call | solution.py:280
  80.7 0.6 copy.5
